TPU v7x, 32 devices: a whole 2x2x4 slice. The times are simulated.
32 devices in a mesh: batch: 16 (over z, y, x), stream: 2 (over core).
Axes of the slice: x: 2, y: 2, z: 4, core: 2. Of those that a mesh axis runs over, the one named last changes fastest.
Arguments:
- tokens: bfloat16 [128, 198, 768], P(('batch', 'stream')), may hold values from -6 to 6
- prompts: float32 [50, 768], replicated, may hold values from -6 to 6
- keep_mask: int32 [128, 196], P(('batch', 'stream')), may hold values from 0 to 1, as said below
- counts: int32 [128], P(('batch', 'stream')), may hold values from 79 to 196, as said below
- ln1_gain: float32 [768], replicated, may hold values from 0.5 to 1.5
- ln1_bias: float32 [768], replicated, may hold values from -0.6 to 0.6
- w_qkv: bfloat16 [768, 2304], replicated, may hold values from -0.21875 to 0.21875
- q_bias: float32 [768], replicated, may hold values from -0.6 to 0.6
- v_bias: float32 [768], replicated, may hold values from -0.6 to 0.6
- w_out: bfloat16 [768, 768], replicated, may hold values from -2.5 to 2.5
- out_bias: float32 [768], replicated, may hold values from -0.6 to 0.6
- ln2_gain: float32 [768], replicated, may hold values from 0.5 to 1.5
- ln2_bias: float32 [768], replicated, may hold values from -0.6 to 0.6
- w_fc1: bfloat16 [768, 3072], replicated, may hold values from -0.21875 to 0.21875
- fc1_bias: float32 [3072], replicated, may hold values from -0.6 to 0.6
- w_fc2: bfloat16 [3072, 768], replicated, may hold values from -0.109375 to 0.109375
- fc2_bias: float32 [768], replicated, may hold values from -0.6 to 0.6
- cot_seq: bfloat16 [128, 198, 768], P(('batch', 'stream')), may hold values from -6 to 6
- cot_prompt: bfloat16 [128, 50, 768], P(('batch', 'stream')), may hold values from -6 to 6
Outputs:
- layer_out: bfloat16 [128, 198, 768], P(('batch', 'stream'))
- prompt_out: bfloat16 [128, 50, 768], P(('batch', 'stream'))
- input_grad: float32 [128, 198, 768], P(('batch', 'stream'))
- prompt_grad: float32 [50, 768], replicated
- penalty: float32 [], replicated
Inputs may be any that keep to these rules, and one draw needn't show every extreme that they name: `keep_mask`: 1 keeps a patch; row i has exactly counts[i] ones. counts[i] is the number of ones in row i of keep_mask.
All inputs are finite; a program needn't handle non-finite values.
Results may differ from a plain program's by a relative error of at most 0.01.
Values sent between devices are 32-bit elements; how exact they have to be, the bound alone decides.
A program may use at most 128 MiB of HBM per device.

v0:
```python
import math
import jax
import jax.numpy as jnp
from jax import lax
from jax.sharding import PartitionSpec as P

HEADS = 12
EPSILON = 1e-06


def layer_norm(values_in, norm_gain, norm_shift):
    row_mean = jnp.mean(values_in, axis=-1, keepdims=True)
    centered = values_in - row_mean
    variance = jnp.mean(centered * centered, axis=-1, keepdims=True)
    return centered * lax.rsqrt(variance + EPSILON) * norm_gain + norm_shift


def split_heads(tensor, head_count):
    return tensor.reshape(
        tensor.shape[0], tensor.shape[1], head_count, tensor.shape[2] // head_count
    )


def masked_scores(queries, key_part, live_keys, head_count, score_scale):
    raw_scores = jnp.einsum(
        "iqhd,ikhd->ihqk",
        split_heads(queries, head_count),
        split_heads(key_part, head_count),
        preferred_element_type=jnp.float32,
    )
    return jnp.where(live_keys[:, None, None, :], raw_scores * score_scale, -1e30)


def project_pairs(pair_grads, pair_weight):
    return jnp.einsum("pe,de->pd", pair_grads, pair_weight, precision=lax.Precision.HIGHEST)


def body(
    tokens,
    prompts,
    keep_mask,
    counts,
    ln1_gain,
    ln1_bias,
    w_qkv,
    q_bias,
    v_bias,
    w_out,
    out_bias,
    ln2_gain,
    ln2_bias,
    w_fc1,
    fc1_bias,
    w_fc2,
    fc2_bias,
    cot_seq,
    cot_prompt,
):
    images, seq_length, model_width = tokens.shape
    prompt_count = prompts.shape[0]
    head_count = HEADS
    score_scale = (model_width // head_count) ** (-0.5)
    total_images = images * lax.axis_size("batch") * lax.axis_size("stream")
    count_sum = jnp.sum(counts.astype(jnp.float32))
    kept_total = lax.psum(count_sum, ("batch", "stream"))
    keep_full = jnp.concatenate(
        [jnp.ones((images, seq_length - keep_mask.shape[1]), jnp.int32), keep_mask], axis=1
    )
    kept_cols = keep_full[:, :, None] > 0
    live_keys = (
        jnp.concatenate([jnp.ones((images, prompt_count), jnp.int32), keep_full], axis=1) > 0
    )
    prompt_normed, prompt_norm_back = jax.vjp(
        lambda rows_in: layer_norm(rows_in, ln1_gain, ln1_bias), prompts
    )
    prompt_proj = jnp.dot(
        prompt_normed.astype(jnp.bfloat16), w_qkv, preferred_element_type=jnp.float32
    )
    prompt_query = (prompt_proj[:, :model_width] + q_bias).astype(jnp.bfloat16)
    prompt_pairs = jnp.concatenate(
        [prompt_proj[:, model_width : 2 * model_width], prompt_proj[:, 2 * model_width :] + v_bias],
        axis=1,
    ).astype(jnp.bfloat16)
    token_rows = tokens.astype(jnp.float32)
    token_normed, token_norm_back = jax.vjp(
        lambda rows_in: layer_norm(rows_in, ln1_gain, ln1_bias), token_rows
    )
    token_proj = jnp.einsum(
        "ihd,de->ihe", token_normed.astype(jnp.bfloat16), w_qkv, preferred_element_type=jnp.float32
    )
    token_query = (token_proj[..., :model_width] + q_bias).astype(jnp.bfloat16)
    token_pairs = jnp.concatenate(
        [
            token_proj[..., model_width : 2 * model_width],
            token_proj[..., 2 * model_width :] + v_bias,
        ],
        axis=2,
    ).astype(jnp.bfloat16)
    queries = jnp.concatenate(
        [jnp.broadcast_to(prompt_query[None], (images, prompt_count, model_width)), token_query],
        axis=1,
    )
    pairs = jnp.concatenate(
        [
            jnp.broadcast_to(prompt_pairs[None], (images, prompt_count, 2 * model_width)),
            token_pairs,
        ],
        axis=1,
    )
    key_part = pairs[..., :model_width]
    value_part = pairs[..., model_width:]
    value_heads = split_heads(value_part, head_count)
    scores = masked_scores(queries, key_part, live_keys, head_count, score_scale)
    top_score = jnp.max(scores, axis=-1, keepdims=True)
    log_total = top_score + jnp.log(jnp.sum(jnp.exp(scores - top_score), axis=-1, keepdims=True))
    soft_low = jnp.exp(scores - log_total).astype(jnp.bfloat16)
    context = jnp.einsum(
        "ihqk,ikhd->iqhd", soft_low, value_heads, preferred_element_type=jnp.float32
    )
    context = context.reshape(images, -1, model_width).astype(jnp.bfloat16)
    attention = (
        jnp.einsum("ird,de->ire", context, w_out, preferred_element_type=jnp.float32) + out_bias
    )
    residual = jnp.concatenate(
        [jnp.broadcast_to(prompts[None], (images, prompt_count, model_width)), token_rows], axis=1
    )
    middle = residual + attention
    second_norm, second_norm_back = jax.vjp(
        lambda rows_in: layer_norm(rows_in, ln2_gain, ln2_bias), middle
    )
    hidden = (
        jnp.einsum(
            "ird,df->irf",
            second_norm.astype(jnp.bfloat16),
            w_fc1,
            preferred_element_type=jnp.float32,
        )
        + fc1_bias
    )
    activated, gelu_back = jax.vjp(lambda rows_in: jax.nn.gelu(rows_in, approximate=False), hidden)
    result = (
        middle
        + jnp.einsum(
            "irf,fd->ird", activated.astype(jnp.bfloat16), w_fc2, preferred_element_type=jnp.float32
        )
        + fc2_bias
    )
    prompt_out = result[:, :prompt_count].astype(jnp.bfloat16)
    layer_out = jnp.where(kept_cols, result[:, prompt_count:], token_rows).astype(jnp.bfloat16)
    grad_result = jnp.concatenate(
        [cot_prompt, jnp.where(kept_cols, cot_seq, jnp.zeros_like(cot_seq))], axis=1
    )
    grad_act = jnp.einsum("ird,fd->irf", grad_result, w_fc2, preferred_element_type=jnp.float32)
    grad_hidden = gelu_back(grad_act)[0].astype(jnp.bfloat16)
    grad_second = jnp.einsum("irf,df->ird", grad_hidden, w_fc1, preferred_element_type=jnp.float32)
    grad_middle = grad_result.astype(jnp.float32) + second_norm_back(grad_second)[0]
    grad_context = jnp.einsum(
        "ire,de->ird", grad_middle.astype(jnp.bfloat16), w_out, preferred_element_type=jnp.float32
    ).astype(jnp.bfloat16)
    again = masked_scores(queries, key_part, live_keys, head_count, score_scale)
    soft_full = jnp.exp(again - log_total)
    soft_back = soft_full.astype(jnp.bfloat16)
    context_heads = split_heads(grad_context, head_count)
    grad_soft = jnp.einsum(
        "iqhd,ikhd->ihqk", context_heads, value_heads, preferred_element_type=jnp.float32
    )
    grad_values = jnp.einsum(
        "ihqk,iqhd->ikhd", soft_back, context_heads, preferred_element_type=jnp.float32
    ).reshape(images, -1, model_width)
    row_dot = jnp.sum(soft_full * grad_soft, axis=-1, keepdims=True)
    grad_scores = (soft_full * (grad_soft - row_dot)).astype(jnp.bfloat16)
    grad_queries = (
        jnp.einsum(
            "ihqk,ikhd->iqhd",
            grad_scores,
            split_heads(key_part, head_count),
            preferred_element_type=jnp.float32,
        )
        * score_scale
    )
    grad_queries = grad_queries.reshape(images, -1, model_width).astype(jnp.bfloat16)
    grad_keys = (
        jnp.einsum(
            "ihqk,iqhd->ikhd",
            grad_scores,
            split_heads(queries, head_count),
            preferred_element_type=jnp.float32,
        )
        * score_scale
    ).reshape(images, -1, model_width)
    grad_pairs = jnp.concatenate([grad_keys, grad_values], axis=2)
    token_proj_grad = jnp.concatenate(
        [grad_queries[:, prompt_count:], grad_pairs[:, prompt_count:].astype(jnp.bfloat16)], axis=2
    )
    grad_token_normed = jnp.einsum(
        "ihe,de->ihd", token_proj_grad, w_qkv, preferred_element_type=jnp.float32
    )
    grad_tokens = grad_middle[:, prompt_count:] + token_norm_back(grad_token_normed)[0]
    input_grad = jnp.where(kept_cols, grad_tokens, cot_seq.astype(jnp.float32))
    pair_weight = w_qkv[:, model_width:].astype(jnp.float32)
    pair_local = jnp.sum(grad_pairs[:, :prompt_count], axis=0)
    query_normed = jnp.sum(
        jnp.einsum(
            "ipe,de->ipd",
            grad_queries[:, :prompt_count],
            w_qkv[:, :model_width],
            preferred_element_type=jnp.float32,
        ),
        axis=0,
    )
    middle_sum = jnp.sum(grad_middle[:, :prompt_count], axis=0)
    prompt_local = prompt_norm_back(query_normed)[0] + middle_sum
    pair_total = lax.psum(pair_local, ("batch", "stream"))
    prompt_total = lax.psum(prompt_local, ("batch", "stream"))
    prompt_total = prompt_total + prompt_norm_back(project_pairs(pair_total, pair_weight))[0]
    penalty_weight = kept_total / (keep_mask.shape[1] * math.sqrt(total_images))
    prompt_grad = prompt_total + 2.0 * penalty_weight * prompts
    penalty = penalty_weight * jnp.sum(prompts * prompts) / (prompt_count * model_width)
    return (layer_out, prompt_out, input_grad, prompt_grad, penalty)


def solution(mesh):
    in_specs = (
        P(("batch", "stream"), None, None),
        P(),
        P(("batch", "stream"), None),
        P(("batch", "stream")),
        P(),
        P(),
        P(),
        P(),
        P(),
        P(),
        P(),
        P(),
        P(),
        P(),
        P(),
        P(),
        P(),
        P(("batch", "stream"), None, None),
        P(("batch", "stream"), None, None),
    )
    out_specs = (
        P(("batch", "stream"), None, None),
        P(("batch", "stream"), None, None),
        P(("batch", "stream"), None, None),
        P(),
        P(),
    )
    return jax.shard_map(body, mesh=mesh, in_specs=in_specs, out_specs=out_specs, check_vma=False)
```

profile of v0, /device:TPU:10, one launch (start us, length us, event | category | flops | bytes accessed | tf_op | source)
XLA Modules:
  0.0 464.4 jit_solution(8597299555711745016)
XLA Ops:
  10.7 5.8 %fusion.29 = f32[4,198,2304]{2,1,0:T(8,128)S(1)} fusion(bf16[768,2304]{1,0:T(8,128)(2,1)} %param.25, f32[768]{0:T(1024)} %param.24, f32[768]{0:T(1024)} %param.23, f32[4,198]{1,0:T(4,128)S(1)} %fusion.73, f32[4,198]{1,0:T(4,128)S(1)} %broadcast_multiply_fusion.1, bf16[4,198,768]{2,0,1:T(4,128)(2,1)} %param.19), kind=kOutput, calls=%fused_computation.49 | convolution fusion | flops 2806493184 | bytes 12067008 | tf_op jit(solution)/shard_map/ihd,de->ihe/dot_general | solution.py:88
  16.5 3.0 copy-done.17
  21.0 2.8 fusion.68
  23.8 4.0 fusion.35
  32.1 2.7 copy.49
  35.0 2.7 pad_maximum_fusion
  37.7 2.6 copy.50
  40.3 2.6 copy.51
  42.9 5.0 %fusion.6 = (f32[4,12,248]{2,1,0:T(8,128)S(1)}, f32[4,12,248,248]{2,3,1,0:T(8,128)S(1)}) fusion(pred[4,248]{1,0:T(4,128)(4,1)S(1)} %add_compare_fusion, bf16[4,248,12,64]{1,3,2,0:T(8,128)(2,1)} %bitcast.72, bf16[4,248,12,64]{1,3,2,0:T(8,128)(2,1)} %bitcast.70), kind=kOutput, calls=%fused_computation.26 | convolution fusion | flops 386725248 | bytes 14904800 | tf_op jit(solution)/shard_map/iqhd,ikhd->ihqk/dot_general | solution.py:25
  47.9 3.4 exponential_reduce_fusion
  52.5 3.1 convolution_convert_fusion
  58.8 13.1 %fusion.32 = (u8[248,3072]{1,0:T(8,128)(4,1)S(1)}, u8[248,3072]{1,0:T(8,128)(4,1)S(1)}, f32[4,248,3072]{2,1,0:T(8,128)}) fusion(f32[3072]{0:T(1024)S(1)} %copy-done.29, bf16[768,3072]{1,0:T(8,128)(2,1)S(1)} %bitcast.83, f32[4,248,768]{2,1,0:T(8,128)S(1)} %get-tuple-element.36, f32[768]{0:T(1024)S(1)} %copy-done.34, f32[768]{0:T(1024)S(1)} %copy-done.25, ...), kind=kOutput, calls=%fused_computation.60 | convolution fusion | flops 4725792768 | bytes 21505792 | tf_op jit(solution)/shard_map/ird,df->irf/dot_general | solution.py:132
  71.9 29.0 %fusion = f32[4,248,3072]{2,1,0:T(8,128)} fusion(f32[4,248,3072]{2,1,0:T(8,128)} %get-tuple-element.37, f32[3072]{0:T(1024)S(1)} %copy-done.29, u8[248,3072]{1,0:T(8,128)(4,1)S(1)} %get-tuple-element.16, u8[248,3072]{1,0:T(8,128)(4,1)S(1)} %get-tuple-element.15), kind=kLoop, calls=%fused_computation.1 | loop fusion | flops 207224832 | bytes 25915392 | tf_op jit(solution)/shard_map/jvp()/erfc | solution.py:140
  100.9 14.7 %add_add_fusion.3 = bf16[4,248,768]{2,1,0:T(8,128)(2,1)S(1)} fusion(f32[4,248,768]{2,1,0:T(8,128)S(1)} %get-tuple-element.36, bf16[3072,768]{1,0:T(8,128)(2,1)} %param.34, f32[4,248,3072]{2,1,0:T(8,128)} %fusion, f32[4,248,3072]{2,1,0:T(8,128)} %get-tuple-element.37, f32[3072]{0:T(1024)S(1)} %copy-done.29, f32[768]{0:T(1024)S(1)} %copy-done.35), kind=kOutput, calls=%fused_computation.56 | convolution fusion | flops 4695318528 | bytes 33684480 | tf_op jit(solution)/shard_map/irf,fd->ird/dot_general | solution.py:143
  117.9 19.5 %multiply_reduce_fusion.1 = (f32[4,248]{1,0:T(4,128)S(1)}, f32[4,248,768]{2,1,0:T(8,128)}) fusion(f32[4,248,768]{2,1,0:T(8,128)} %copy-done.4, f32[768]{0:T(1024)S(1)} %copy-done.25, f32[4,248]{1,0:T(4,128)S(1)} %broadcast_multiply_fusion, bf16[768,3072]{1,0:T(8,128)(2,1)} %param.32, f32[4,248,3072]{2,1,0:T(8,128)} %fusion, ...), kind=kOutput, calls=%fused_computation.55 | convolution fusion | flops 9413491712 | bytes 41458432 | tf_op jit(solution)/shard_map/irf,df->ird/dot_general | solution.py:155
  137.5 3.5 fusion.60
  146.2 2.6 convolution_convert_fusion.1
  148.8 2.6 copy.56
  151.5 14.3 %multiply_reduce_fusion = (f32[4,12,248]{2,1,0:T(8,128)S(1)}, f32[4,12,248,248]{2,3,1,0:T(8,128)}) fusion(f32[4,12,248,248]{2,3,1,0:T(8,128)} %copy-done.1, f32[4,12,248]{2,1,0:T(8,128)S(1)} %log_add_fusion, pred[4,248]{1,0:T(4,128)(4,1)S(1)} %add_compare_fusion, bf16[4,248,12,64]{1,3,2,0:T(8,128)(2,1)} %bitcast.74, bf16[4,248,12,64]{1,3,2,0:T(8,128)(2,1)} %bitcast.80), kind=kOutput, calls=%fused_computation.8 | convolution fusion | flops 392629632 | bytes 26761184 | tf_op jit(solution)/shard_map/iqhd,ikhd->ihqk/dot_general | solution.py:164
  165.8 9.0 %fusion.64 = f32[4,12,64,248]{3,2,1,0:T(8,128)} fusion(bf16[4,248,12,64]{1,3,2,0:T(8,128)(2,1)S(1)} %bitcast.75, f32[4,12,248,248]{2,3,1,0:T(8,128)} %copy-done.1, f32[4,12,248]{2,1,0:T(8,128)S(1)} %log_add_fusion, pred[4,248]{1,0:T(4,128)(4,1)S(1)} %add_compare_fusion), kind=kOutput, calls=%fused_computation.121 | convolution fusion | flops 389689344 | bytes 16428512 | tf_op jit(solution)/shard_map/ihqk,iqhd->ikhd/dot_general | solution.py:167
  174.8 6.9 %multiply_convert_fusion = bf16[4,12,248,248]{2,3,1,0:T(8,128)(2,1)S(1)} fusion(f32[4,12,248,248]{2,3,1,0:T(8,128)} %get-tuple-element.41, f32[4,12,248,248]{2,3,1,0:T(8,128)S(1)} %bitcast.69, f32[4,12,248]{2,1,0:T(8,128)S(1)} %get-tuple-element.40, f32[4,12,248]{2,1,0:T(8,128)S(1)} %log_add_fusion, pred[4,248]{1,0:T(4,128)(4,1)S(1)} %add_compare_fusion), kind=kLoop, calls=%fused_computation.7 | loop fusion | flops 17713152 | bytes 29618144 | tf_op jit(solution)/shard_map/convert_element_type | solution.py:171
  181.8 3.7 convolution_multiply_fusion
  185.5 3.5 copy.61
  189.0 3.6 copy.62
  195.1 4.5 fusion.13
  199.6 4.0 multiply_convert_fusion.3
  209.0 6.3 %multiply_reduce_fusion.3 = (f32[4,198]{1,0:T(4,128)S(1)}, f32[4,198,768]{2,1,0:T(8,128)S(1)}) fusion(f32[768]{0:T(1024)S(1)} %copy-done.24, f32[4,198]{1,0:T(4,128)S(1)} %broadcast_multiply_fusion.1, bf16[4,198,768]{2,0,1:T(4,128)(2,1)S(1)} %copy-done.3, bf16[768,2304]{1,0:T(8,128)(2,1)} %param.25, bf16[4,198,1536]{2,1,0:T(8,128)(2,1)} %fusion.13, ...), kind=kOutput, calls=%fused_computation.70 | convolution fusion | flops 2813183232 | bytes 10847424 | tf_op jit(solution)/shard_map/ihe,de->ihd/dot_general | solution.py:195
  222.3 41.6 %psum.23 = f32[]{:T(128)} all-reduce(f32[]{:T(128)} %convert_reduce_fusion.1), channel_id=1, replica_groups=mesh['batch'=16,'stream'=2] {'batch','stream'}, use_global_device_ids=true, to_apply=%region_23.24 | all-reduce | flops 1 | bytes 8 | tf_op jit(solution)/shard_map/psum | solution.py:65
  263.9 2.9 copy.65
  272.5 51.0 %all-reduce.6.cloned.1.call-done = f32[50,1536]{1,0:T(8,128)} async-done(((f32[50,1536]{1,0:T(8,128)}), f32[50,1536]{1,0:T(8,128)}) %all-reduce.6.cloned.1.call-update) | async-done | bytes 307216 | tf_op jit(solution)/shard_map/psum | solution.py:213
  323.6 4.6 multiply_reduce_fusion.5
  330.0 124.4 %all-reduce.4.cloned.1.call-done = f32[50,768]{1,0:T(8,128)} async-done(((f32[50,768]{1,0:T(8,128)}), f32[50,768]{1,0:T(8,128)}) %all-reduce.4.cloned.1.call-update) | async-done | bytes 153616 | tf_op jit(solution)/shard_map/psum | solution.py:214
  (144 shorter events, 43.4 us)
Async XLA Ops:
  7.2 48.5 %copy-start = (bf16[768,768]{1,0:T(8,128)(2,1)S(1)}, bf16[768,768]{1,0:T(8,128)(2,1)}, u32[]{:S(2)}) copy-start(bf16[768,768]{1,0:T(8,128)(2,1)} %param.28) | copy-start | bytes 3538948
  7.2 316.4 %all-reduce.6.cloned.1.call-start = ((), (), s32[]{:S(2)}) async-start(), calls=%async_computation.1 | async-start | bytes 688128 | tf_op jit(solution)/shard_map/psum | solution.py:213
  10.6 10.0 %copy-start.12 = (f32[50,768]{1,0:T(8,128)S(1)}, f32[50,768]{1,0:T(8,128)}, u32[]{:S(2)}) copy-start(f32[50,768]{1,0:T(8,128)} %param.20) | copy-start | bytes 460804
  10.6 10.3 %copy-start.24 = (f32[768]{0:T(1024)S(1)}, f32[768]{0:T(1024)}, u32[]{:S(2)}) copy-start(f32[768]{0:T(1024)} %param.23) | copy-start | bytes 9220
  10.7 10.3 %copy-start.30 = (f32[768]{0:T(1024)S(1)}, f32[768]{0:T(1024)}, u32[]{:S(2)}) copy-start(f32[768]{0:T(1024)} %param.24) | copy-start | bytes 9220
  19.5 4.3 copy-start.26
  19.5 4.3 copy-start.27
  23.8 4.1 copy-start.3
  47.9 4.6 copy-start.1
  47.9 4.6 copy-start.16
  52.5 3.2 copy-start.21
  52.5 3.2 copy-start.33
  55.6 3.1 slice-start.4
  55.7 3.0 slice-start.5
  57.5 43.4 %copy-start.4 = (f32[4,248,768]{2,1,0:T(8,128)}, f32[4,248,768]{2,1,0:T(8,128)S(1)}, u32[]{:S(2)}) copy-start(f32[4,248,768]{2,1,0:T(8,128)S(1)} %get-tuple-element.36) | copy-start | bytes 9142276
  71.9 29.0 %copy-start.35 = (f32[768]{0:T(1024)S(1)}, f32[768]{0:T(1024)}, u32[]{:S(2)}) copy-start(f32[768]{0:T(1024)} %param.35) | copy-start | bytes 9220
  100.9 14.7 %copy-start.19 = (bf16[4,198,768]{2,0,1:T(4,128)(2,1)S(1)}, bf16[4,198,768]{2,0,1:T(4,128)(2,1)}, u32[]{:S(2)}) copy-start(bf16[4,198,768]{2,0,1:T(4,128)(2,1)} %param.36) | copy-start | bytes 3649540
  137.5 3.7 copy-start.5
  137.5 4.6 copy-start.11
  151.5 14.4 %copy-start.8 = (bf16[4,248,768]{1,2,0:T(8,128)(2,1)S(1)}, bf16[4,248,768]{1,2,0:T(8,128)(2,1)}, u32[]{:S(2)}) copy-start(bf16[4,248,768]{1,2,0:T(8,128)(2,1)} %copy.56) | copy-start | bytes 4571140
  151.5 23.4 %slice-start = ((s8[12189696]{0:T(1024)(128)(4,1)}), s8[4194304]{0:T(1024)(128)(4,1)S(1)}, s32[]{:S(2)}) async-start(s8[12189696]{0:T(1024)(128)(4,1)} %bitcast.68), calls=%async_computation.2 | async-start | bytes 8388608
  151.5 23.4 %slice-start.1 = ((s8[12189696]{0:T(1024)(128)(4,1)}), s8[3801088]{0:T(1024)(128)(4,1)S(1)}, s32[]{:S(2)}) async-start(s8[12189696]{0:T(1024)(128)(4,1)} %bitcast.68), calls=%async_computation.3 | async-start | bytes 7602176
  165.8 9.0 %slice-start.2 = ((s8[12189696]{0:T(1024)(128)(4,1)}), s8[4194304]{0:T(1024)(128)(4,1)S(1)}, s32[]{:S(2)}) async-start(s8[12189696]{0:T(1024)(128)(4,1)} %bitcast.68), calls=%async_computation.4 | async-start | bytes 8388608
  174.8 7.0 %copy-start.7 = (bf16[4,248,768]{1,2,0:T(8,128)(2,1)S(1)}, bf16[4,248,768]{1,2,0:T(8,128)(2,1)}, u32[]{:S(2)}) copy-start(bf16[4,248,768]{1,2,0:T(8,128)(2,1)} %copy.50) | copy-start | bytes 4571140
  181.8 3.7 copy-start.2
  194.8 259.7 %all-reduce.4.cloned.1.call-start = ((), (), s32[]{:S(2)}) async-start(), calls=%async_computation | async-start | bytes 344064 | tf_op jit(solution)/shard_map/psum | solution.py:214
  195.1 4.6 copy-start.6
  209.0 7.3 %copy-start.20 = (bf16[4,198,768]{2,0,1:T(4,128)(2,1)S(1)}, bf16[4,198,768]{2,0,1:T(4,128)(2,1)}, u32[]{:S(2)}) copy-start(bf16[4,198,768]{2,0,1:T(4,128)(2,1)} %param.36) | copy-start | bytes 3649540
  217.2 3.0 copy-start.15
  220.2 46.6 %slice-start.3 = ((bf16[4,248,768]{2,1,0:T(8,128)(2,1)}), bf16[4,50,768]{2,1,0:T(8,128)(2,1)S(1)}, s32[]{:S(2)}) async-start(bf16[4,248,768]{2,1,0:T(8,128)(2,1)} %copy-done.22), calls=%async_computation.5 | async-start | bytes 688128 | tf_op jit(solution)/shard_map/slice | solution.py:148
  263.9 3.8 copy-start.13
  270.1 58.1 %copy-start.32 = (f32[50]{0:T(128)S(1)}, f32[50]{0:T(128)}, u32[]{:S(2)}) copy-start(f32[50]{0:T(128)} %copy-done.31) | copy-start | bytes 604
  (13 other events, 23.8 us)
Sparse Core Ops, SparseCore 0:
  194.9 128.5 all-reduce.5
  330.6 123.8 all-reduce.3
where the time goes:
time: 470 us; the launch traced here: 464 us
  waiting for transfers between devices  175 us (37%)
  matrix products  112 us (24%)
  other arithmetic  75.7 us (16%)
  blocking collectives  41.6 us (9%)
  local copies, waits for them, and re-layouts  41.1 us (9%)
  between operations  17.9 us (4%)
    psum x1, waiting for transfers between devices, body(): prompt_total = lax.psum(prompt_local, ('batch', 'stream'))  124 us
    psum x1, waiting for transfers between devices, body(): pair_total = lax.psum(pair_local, ('batch', 'stream'))  51 us
    psum x1, blocking collectives, body(): kept_total = lax.psum(count_sum, ('batch', 'stream'))  41.6 us
    another operation x1, other arithmetic, body(): jax.nn.gelu(rows_in, approximate=False)  29 us
    dot_general x1, matrix products, body(): jnp.einsum('irf,df->ird', grad_hidden, w_fc1, preferred_element_type=jnp....  19.5 us
    unnamed x89, local copies, waits for them, and re-layouts  18.5 us
    dot_general x1, matrix products, body(): jnp.einsum('irf,fd->ird', activated.astype(jnp.bfloat16), w_fc2, preferre...  14.7 us
    dot_general x1, matrix products, body(): jnp.einsum('iqhd,ikhd->ihqk', context_heads, value_heads, preferred_eleme...  14.3 us
  transfers between devices with their start and end apart: 2, of which 2 were waited for; matrix products, arithmetic and copies ran while one was open for 7% of the time, Pallas kernels for 0%

commit v1 on v0

--- a/solution.py
+++ b/solution.py
@@ -211,7 +211,7 @@
     middle_sum = jnp.sum(grad_middle[:, :prompt_count], axis=0)
     prompt_local = prompt_norm_back(query_normed)[0] + middle_sum
     pair_total = lax.psum(pair_local, ("batch", "stream"))
-    prompt_total = lax.psum(prompt_local, ("batch", "stream"))
+    prompt_total = jnp.sum(lax.all_gather(prompt_local, ("batch", "stream")), axis=0)
     prompt_total = prompt_total + prompt_norm_back(project_pairs(pair_total, pair_weight))[0]
     penalty_weight = kept_total / (keep_mask.shape[1] * math.sqrt(total_images))
     prompt_grad = prompt_total + 2.0 * penalty_weight * prompts

time: 470 us -> 413 us (0.88)
  waiting for transfers between devices: 175 us -> 122 us
    psum x1 -> x0, waiting for transfers between devices: 124 us -> none  [body(): prompt_total = lax.psum(prompt_local, ('batch', 'stream'))]
    psum x1, waiting for transfers between devices: 51 us -> 120 us  [body(): pair_total = lax.psum(pair_local, ('batch', 'stream'))]
where the time goes in v1:
time: 413 us; the launch traced here: 407 us
  waiting for transfers between devices  122 us (30%)
  matrix products  110 us (27%)
  other arithmetic  75.2 us (18%)
  local copies, waits for them, and re-layouts  42.1 us (10%)
  blocking collectives  39.6 us (10%)
  between operations  17.7 us (4%)
    psum x1, waiting for transfers between devices, body(): pair_total = lax.psum(pair_local, ('batch', 'stream'))  120 us
    psum x1, blocking collectives, body(): kept_total = lax.psum(count_sum, ('batch', 'stream'))  39.6 us
    another operation x1, other arithmetic, body(): jax.nn.gelu(rows_in, approximate=False)  29 us
    dot_general x1, matrix products, body(): jnp.einsum('irf,df->ird', grad_hidden, w_fc1, preferred_element_type=jnp....  19.5 us
    unnamed x89, local copies, waits for them, and re-layouts  17.9 us
    dot_general x1, matrix products, body(): jnp.einsum('irf,fd->ird', activated.astype(jnp.bfloat16), w_fc2, preferre...  14.7 us
    dot_general x1, matrix products, body(): jnp.einsum('iqhd,ikhd->ihqk', context_heads, value_heads, preferred_eleme...  14.4 us
    dot_general x1, matrix products, body(): jnp.einsum('ird,df->irf', second_norm.astype(jnp.bfloat16), w_fc1, prefer...  13.1 us
  transfers between devices with their start and end apart: 2, of which 2 were waited for; matrix products, arithmetic and copies ran while one was open for 7% of the time, Pallas kernels for 0%

profile of v1, /device:TPU:10, one launch (start us, length us, event | category | flops | bytes accessed | tf_op | source)
XLA Modules:
  0.0 407.0 jit_solution(8998295568785090678)
XLA Ops:
  10.7 5.8 %fusion.29 = f32[4,198,2304]{2,1,0:T(8,128)S(1)} fusion(bf16[768,2304]{1,0:T(8,128)(2,1)} %param.25, f32[768]{0:T(1024)} %param.24, f32[768]{0:T(1024)} %param.23, f32[4,198]{1,0:T(4,128)S(1)} %fusion.73, f32[4,198]{1,0:T(4,128)S(1)} %broadcast_multiply_fusion.1, bf16[4,198,768]{2,0,1:T(4,128)(2,1)} %param.19), kind=kOutput, calls=%fused_computation.49 | convolution fusion | flops 2806493184 | bytes 12067008 | tf_op jit(solution)/shard_map/ihd,de->ihe/dot_general | solution.py:88
  16.5 3.0 copy-done.15
  21.0 2.8 fusion.68
  23.8 4.0 fusion.35
  32.1 2.7 copy.69
  35.1 2.7 pad_maximum_fusion
  40.3 2.6 copy.71
  42.9 5.0 %fusion.6 = (f32[4,12,248]{2,1,0:T(8,128)S(1)}, f32[4,12,248,248]{2,3,1,0:T(8,128)S(1)}) fusion(pred[4,248]{1,0:T(4,128)(4,1)S(1)} %add_compare_fusion, bf16[4,248,12,64]{1,3,2,0:T(8,128)(2,1)} %bitcast.74, bf16[4,248,12,64]{1,3,2,0:T(8,128)(2,1)} %bitcast.72), kind=kOutput, calls=%fused_computation.26 | convolution fusion | flops 386725248 | bytes 14904800 | tf_op jit(solution)/shard_map/iqhd,ikhd->ihqk/dot_general | solution.py:25
  48.0 3.4 exponential_reduce_fusion
  52.5 3.1 convolution_convert_fusion
  58.9 13.1 %fusion.32 = (u8[248,3072]{1,0:T(8,128)(4,1)S(1)}, u8[248,3072]{1,0:T(8,128)(4,1)S(1)}, f32[4,248,3072]{2,1,0:T(8,128)}) fusion(f32[3072]{0:T(1024)S(1)} %copy-done.31, bf16[768,3072]{1,0:T(8,128)(2,1)S(1)} %bitcast.85, f32[4,248,768]{2,1,0:T(8,128)S(1)} %get-tuple-element.41, f32[768]{0:T(1024)S(1)} %copy-done.34, f32[768]{0:T(1024)S(1)} %copy-done.27, ...), kind=kOutput, calls=%fused_computation.60 | convolution fusion | flops 4725792768 | bytes 21505792 | tf_op jit(solution)/shard_map/ird,df->irf/dot_general | solution.py:132
  71.9 29.0 %fusion = f32[4,248,3072]{2,1,0:T(8,128)} fusion(f32[4,248,3072]{2,1,0:T(8,128)} %get-tuple-element.42, f32[3072]{0:T(1024)S(1)} %copy-done.31, u8[248,3072]{1,0:T(8,128)(4,1)S(1)} %get-tuple-element.21, u8[248,3072]{1,0:T(8,128)(4,1)S(1)} %get-tuple-element.20), kind=kLoop, calls=%fused_computation.1 | loop fusion | flops 207224832 | bytes 25915392 | tf_op jit(solution)/shard_map/jvp()/erfc | solution.py:140
  101.0 14.7 %add_add_fusion.3 = bf16[4,248,768]{2,1,0:T(8,128)(2,1)S(1)} fusion(f32[4,248,768]{2,1,0:T(8,128)S(1)} %get-tuple-element.41, bf16[3072,768]{1,0:T(8,128)(2,1)} %param.34, f32[4,248,3072]{2,1,0:T(8,128)} %fusion, f32[4,248,3072]{2,1,0:T(8,128)} %get-tuple-element.42, f32[3072]{0:T(1024)S(1)} %copy-done.31, f32[768]{0:T(1024)S(1)} %copy-done.35), kind=kOutput, calls=%fused_computation.56 | convolution fusion | flops 4695318528 | bytes 33684480 | tf_op jit(solution)/shard_map/irf,fd->ird/dot_general | solution.py:143
  117.9 19.5 %multiply_reduce_fusion.1 = (f32[4,248]{1,0:T(4,128)S(1)}, f32[4,248,768]{2,1,0:T(8,128)}) fusion(f32[4,248,768]{2,1,0:T(8,128)} %copy-done.4, f32[768]{0:T(1024)S(1)} %copy-done.27, f32[4,248]{1,0:T(4,128)S(1)} %broadcast_multiply_fusion, bf16[768,3072]{1,0:T(8,128)(2,1)} %param.32, f32[4,248,3072]{2,1,0:T(8,128)} %fusion, ...), kind=kOutput, calls=%fused_computation.55 | convolution fusion | flops 9413491712 | bytes 41458432 | tf_op jit(solution)/shard_map/irf,df->ird/dot_general | solution.py:155
  137.5 3.5 fusion.60
  146.2 2.6 convolution_convert_fusion.1
  148.8 2.6 copy.76
  151.5 14.4 %multiply_reduce_fusion = (f32[4,12,248]{2,1,0:T(8,128)S(1)}, f32[4,12,248,248]{2,3,1,0:T(8,128)}) fusion(f32[4,12,248,248]{2,3,1,0:T(8,128)} %copy-done.1, f32[4,12,248]{2,1,0:T(8,128)S(1)} %log_add_fusion, pred[4,248]{1,0:T(4,128)(4,1)S(1)} %add_compare_fusion, bf16[4,248,12,64]{1,3,2,0:T(8,128)(2,1)} %bitcast.76, bf16[4,248,12,64]{1,3,2,0:T(8,128)(2,1)} %bitcast.82), kind=kOutput, calls=%fused_computation.8 | convolution fusion | flops 392629632 | bytes 26761184 | tf_op jit(solution)/shard_map/iqhd,ikhd->ihqk/dot_general | solution.py:164
  165.8 9.0 %fusion.64 = f32[4,12,64,248]{3,2,1,0:T(8,128)} fusion(bf16[4,248,12,64]{1,3,2,0:T(8,128)(2,1)S(1)} %bitcast.77, f32[4,12,248,248]{2,3,1,0:T(8,128)} %copy-done.1, f32[4,12,248]{2,1,0:T(8,128)S(1)} %log_add_fusion, pred[4,248]{1,0:T(4,128)(4,1)S(1)} %add_compare_fusion), kind=kOutput, calls=%fused_computation.121 | convolution fusion | flops 389689344 | bytes 16428512 | tf_op jit(solution)/shard_map/ihqk,iqhd->ikhd/dot_general | solution.py:167
  174.9 6.9 %multiply_convert_fusion = bf16[4,12,248,248]{2,3,1,0:T(8,128)(2,1)S(1)} fusion(f32[4,12,248,248]{2,3,1,0:T(8,128)} %get-tuple-element.46, f32[4,12,248,248]{2,3,1,0:T(8,128)S(1)} %bitcast.71, f32[4,12,248]{2,1,0:T(8,128)S(1)} %get-tuple-element.45, f32[4,12,248]{2,1,0:T(8,128)S(1)} %log_add_fusion, pred[4,248]{1,0:T(4,128)(4,1)S(1)} %add_compare_fusion), kind=kLoop, calls=%fused_computation.7 | loop fusion | flops 17713152 | bytes 29618144 | tf_op jit(solution)/shard_map/convert_element_type | solution.py:171
  181.8 3.7 convolution_multiply_fusion
  185.5 3.5 copy.81
  189.0 3.6 copy.82
  195.1 4.4 %multiply_convert_fusion.3 = bf16[4,12,64,248]{3,2,1,0:T(8,128)(2,1)S(1)} fusion(bf16[4,248,12,64]{1,3,2,0:T(8,128)(2,1)} %bitcast.73, bf16[4,12,248,248]{2,3,1,0:T(8,128)(2,1)} %copy-done.2), kind=kOutput, calls=%fused_computation.51 | convolution fusion | flops 379404288 | bytes 8951808 | tf_op jit(solution)/shard_map/ihqk,ikhd->iqhd/dot_general | solution.py:173
  203.9 119.7 %all-reduce.3.cloned.1.call-done = f32[50,1536]{1,0:T(8,128)} async-done(((f32[50,1536]{1,0:T(8,128)}), f32[50,1536]{1,0:T(8,128)}) %all-reduce.3.cloned.1.call-update) | async-done | bytes 307216 | tf_op jit(solution)/shard_map/psum | solution.py:213
  323.6 4.6 %multiply_reduce_fusion.5 = (f32[]{:T(128)}, f32[50]{0:T(128)S(1)}, f32[50,768]{1,0:T(8,128)S(1)}) fusion(f32[50,768]{1,0:T(8,128)S(1)} %copy-done.11, f32[50]{0:T(128)S(1)} %broadcast_multiply_fusion.2, f32[768]{0:T(1024)S(1)} %copy-done.24, f32[50,1536]{1,0:T(8,128)} %all-reduce.3.cloned.1.call-done, bf16[768,2304]{1,0:T(8,128)(2,1)} %param.25), kind=kOutput, calls=%fused_computation.114 | convolution fusion | flops 708019136 | bytes 3014036 | tf_op jit(solution)/shard_map/pe,de->pd/dot_general | solution.py:35
  330.0 39.6 %psum.15 = f32[]{:T(128)} all-reduce(f32[]{:T(128)} %convert_reduce_fusion.1), channel_id=1, replica_groups=mesh['batch'=16,'stream'=2] {'batch','stream'}, use_global_device_ids=true, to_apply=%region_23.24 | all-reduce | flops 1 | bytes 8 | tf_op jit(solution)/shard_map/psum | solution.py:65
  369.6 3.5 slice.87
  377.9 3.1 fusion.13
  381.8 3.3 multiply_reduce_fusion.3
  392.5 2.7 all-gather.4.cloned.1.call-done
  395.2 2.8 reduce_sum.246
  (145 shorter events, 44.4 us)
Async XLA Ops:
  7.2 48.6 %copy-start = (bf16[768,768]{1,0:T(8,128)(2,1)S(1)}, bf16[768,768]{1,0:T(8,128)(2,1)}, u32[]{:S(2)}) copy-start(bf16[768,768]{1,0:T(8,128)(2,1)} %param.28) | copy-start | bytes 3538948
  7.2 316.4 %all-reduce.3.cloned.1.call-start = ((), (), s32[]{:S(2)}) async-start(), calls=%async_computation | async-start | bytes 688128 | tf_op jit(solution)/shard_map/psum | solution.py:213
  10.6 5.9 %copy-start.25 = (f32[4,198]{1,0:T(4,128)}, f32[4,198]{1,0:T(4,128)S(1)}, u32[]{:S(2)}) copy-start(f32[4,198]{1,0:T(4,128)S(1)} %multiply_reduce_fusion.4) | copy-start | bytes 9508
  10.6 10.0 %copy-start.11 = (f32[50,768]{1,0:T(8,128)S(1)}, f32[50,768]{1,0:T(8,128)}, u32[]{:S(2)}) copy-start(f32[50,768]{1,0:T(8,128)} %param.20) | copy-start | bytes 460804
  10.7 10.3 %copy-start.24 = (f32[768]{0:T(1024)S(1)}, f32[768]{0:T(1024)}, u32[]{:S(2)}) copy-start(f32[768]{0:T(1024)} %param.23) | copy-start | bytes 9220
  10.7 10.3 %copy-start.32 = (f32[768]{0:T(1024)S(1)}, f32[768]{0:T(1024)}, u32[]{:S(2)}) copy-start(f32[768]{0:T(1024)} %param.24) | copy-start | bytes 9220
  19.5 4.3 %copy-start.28 = (f32[768]{0:T(1024)S(1)}, f32[768]{0:T(1024)}, u32[]{:S(2)}) copy-start(f32[768]{0:T(1024)} %param.26) | copy-start | bytes 9220
  19.5 4.3 %copy-start.29 = (f32[768]{0:T(1024)S(1)}, f32[768]{0:T(1024)}, u32[]{:S(2)}) copy-start(f32[768]{0:T(1024)} %param.27) | copy-start | bytes 9220
  23.8 4.1 copy-start.3
  47.9 4.6 %copy-start.1 = (f32[4,12,248,248]{2,3,1,0:T(8,128)}, f32[4,12,248,248]{2,3,1,0:T(8,128)S(1)}, u32[]{:S(2)}) copy-start(f32[4,12,248,248]{2,3,1,0:T(8,128)S(1)} %get-tuple-element.39) | copy-start | bytes 35426308
  47.9 4.6 %copy-start.14 = (bf16[4,248,768]{1,2,0:T(8,128)(2,1)S(1)}, bf16[4,248,768]{1,2,0:T(8,128)(2,1)}, u32[]{:S(2)}) copy-start(bf16[4,248,768]{1,2,0:T(8,128)(2,1)} %copy.69) | copy-start | bytes 4571140
  52.5 3.2 copy-start.20
  52.5 3.2 copy-start.33
  57.5 43.4 %copy-start.4 = (f32[4,248,768]{2,1,0:T(8,128)}, f32[4,248,768]{2,1,0:T(8,128)S(1)}, u32[]{:S(2)}) copy-start(f32[4,248,768]{2,1,0:T(8,128)S(1)} %get-tuple-element.41) | copy-start | bytes 9142276
  71.9 29.0 %copy-start.35 = (f32[768]{0:T(1024)S(1)}, f32[768]{0:T(1024)}, u32[]{:S(2)}) copy-start(f32[768]{0:T(1024)} %param.35) | copy-start | bytes 9220
  100.9 14.7 %copy-start.18 = (bf16[4,198,768]{2,0,1:T(4,128)(2,1)S(1)}, bf16[4,198,768]{2,0,1:T(4,128)(2,1)}, u32[]{:S(2)}) copy-start(bf16[4,198,768]{2,0,1:T(4,128)(2,1)} %param.36) | copy-start | bytes 3649540
  137.5 3.7 copy-start.5
  137.5 4.6 %copy-start.10 = (f32[4,248,768]{2,1,0:T(8,128)S(1)}, f32[4,248,768]{2,1,0:T(8,128)}, u32[]{:S(2)}) copy-start(f32[4,248,768]{2,1,0:T(8,128)} %get-tuple-element.44) | copy-start | bytes 9142276
  151.5 14.4 %copy-start.7 = (bf16[4,248,768]{1,2,0:T(8,128)(2,1)S(1)}, bf16[4,248,768]{1,2,0:T(8,128)(2,1)}, u32[]{:S(2)}) copy-start(bf16[4,248,768]{1,2,0:T(8,128)(2,1)} %copy.76) | copy-start | bytes 4571140
  151.5 23.4 %slice-start = ((s8[12189696]{0:T(1024)(128)(4,1)}), s8[4194304]{0:T(1024)(128)(4,1)S(1)}, s32[]{:S(2)}) async-start(s8[12189696]{0:T(1024)(128)(4,1)} %bitcast.70), calls=%async_computation.2 | async-start | bytes 8388608
  151.5 23.4 %slice-start.1 = ((s8[12189696]{0:T(1024)(128)(4,1)}), s8[3801088]{0:T(1024)(128)(4,1)S(1)}, s32[]{:S(2)}) async-start(s8[12189696]{0:T(1024)(128)(4,1)} %bitcast.70), calls=%async_computation.3 | async-start | bytes 7602176
  165.8 9.0 %slice-start.2 = ((s8[12189696]{0:T(1024)(128)(4,1)}), s8[4194304]{0:T(1024)(128)(4,1)S(1)}, s32[]{:S(2)}) async-start(s8[12189696]{0:T(1024)(128)(4,1)} %bitcast.70), calls=%async_computation.4 | async-start | bytes 8388608
  174.8 7.0 %copy-start.6 = (bf16[4,248,768]{1,2,0:T(8,128)(2,1)S(1)}, bf16[4,248,768]{1,2,0:T(8,128)(2,1)}, u32[]{:S(2)}) copy-start(bf16[4,248,768]{1,2,0:T(8,128)(2,1)} %copy.70) | copy-start | bytes 4571140
  181.8 3.7 copy-start.2
  194.8 200.4 %all-gather.4.cloned.1.call-start = ((), (), s32[]{:S(2)}) async-start(), calls=%async_computation.1 | async-start | bytes 5677056 | tf_op jit(solution)/shard_map/all_gather | solution.py:214
  202.7 126.7 %copy-start.36 = (s32[4]{0:T(128)S(1)}, s32[4]{0:T(128)}, u32[]{:S(2)}) copy-start(s32[4]{0:T(128)} %param.22) | copy-start | bytes 52
  369.6 3.5 copy-start.16
  369.6 5.0 %slice-start.3 = ((bf16[4,248,768]{2,1,0:T(8,128)(2,1)}), bf16[4,50,768]{2,1,0:T(8,128)(2,1)S(1)}, s32[]{:S(2)}) async-start(bf16[4,248,768]{2,1,0:T(8,128)(2,1)} %copy-done.21), calls=%async_computation.5 | async-start | bytes 688128 | tf_op jit(solution)/shard_map/slice | solution.py:148
  377.9 3.5 copy-start.12
  377.9 3.9 copy-start.22
  381.8 3.3 copy-start.26
  381.8 4.3 %copy-start.19 = (bf16[4,198,768]{2,0,1:T(4,128)(2,1)S(1)}, bf16[4,198,768]{2,0,1:T(4,128)(2,1)}, u32[]{:S(2)}) copy-start(bf16[4,198,768]{2,0,1:T(4,128)(2,1)} %param.36) | copy-start | bytes 3649540
  (13 other events, 24.8 us)
Sparse Core Ops, SparseCore 0:
  194.9 128.5 all-reduce.2
  329.5 65.6 all-gather.3
